TPU v7x, 512 devices: a whole 4x4x16 slice. The times are simulated.
512 devices in a mesh: wide: 64 (over z, y_hi, core), narrow: 8 (over x, y_lo).
Axes of the slice: x: 4, y: 4 (y_hi: 2, y_lo: 2; y = y_hi * 2 + y_lo), z: 16, core: 2. Of those that a mesh axis runs over, the one named last changes fastest.
Arguments:
- tokens: bfloat16 [512, 8192], P('wide', 'narrow'), may hold values from -6 to 6
- cotangent: bfloat16 [512, 8192], P('wide', 'narrow'), may hold values from -2.390625 to 2.390625
- gate_vals: bfloat16 [8, 64, 12, 128, 128], P('narrow', 'wide'), may hold values from -0.125 to 0.125
- up_vals: bfloat16 [8, 64, 12, 128, 128], P('narrow', 'wide'), may hold values from -0.125 to 0.125
- gu_index: int32 [8, 64, 12], P('narrow', 'wide'), may hold values from 0 to 15, as said below
- gu_count: int32 [8, 64], P('narrow', 'wide'), may hold values from 1 to 12, as said below
- down_vals: bfloat16 [64, 8, 12, 128, 128], P('wide', 'narrow'), may hold values from -0.09375 to 0.09375
- down_index: int32 [64, 8, 12], P('wide', 'narrow'), may hold values from 0 to 15, as said below
- down_count: int32 [64, 8], P('wide', 'narrow'), may hold values from 1 to 12, as said below
Outputs:
- d_tokens: bfloat16 [512, 8192], P('wide', 'narrow')
- gate_grad: bfloat16 [8, 64, 12, 128, 128], P('narrow', 'wide')
- up_grad: bfloat16 [8, 64, 12, 128, 128], P('narrow', 'wide')
- down_grad: bfloat16 [64, 8, 12, 128, 128], P('wide', 'narrow')
Inputs may be any that keep to these rules, and one draw needn't show every extreme that they name: `gu_index`: within each tile all 12 entries are different. `gu_count`: some tile has exactly 12 live slots. `down_index`: within each tile all 12 entries are different. `down_count`: some tile has exactly 12 live slots.
All inputs are finite; a program needn't handle non-finite values.
Results may differ from a plain program's by a relative error of at most 0.005.
Values may be sent and summed in bfloat16 or wider, within the bound.
A program may use at most 64 MiB of HBM per device.

v0:
```python
import jax
import jax.numpy as jnp
from jax import lax
from jax.sharding import PartitionSpec as P

FF = 16384


def apply_blocks(inputs, tile_values, source_blocks, target_blocks, target_total, form):
    block_size = tile_values.shape[-1]
    row_total = inputs.shape[0]
    pieces = inputs.reshape(row_total, inputs.shape[1] // block_size, block_size)
    picked = jnp.take(pieces, source_blocks, axis=1)
    products = jnp.einsum(form, picked, tile_values, preferred_element_type=jnp.float32)
    placer = (target_blocks[:, None] == jnp.arange(target_total, dtype=jnp.int32)[None, :]).astype(
        jnp.float32
    )
    placed = jnp.einsum("rsn,sc->rcn", products, placer, precision=lax.Precision.HIGHEST)
    return placed.reshape(row_total, target_total * block_size)


def block_grads(left, right, left_blocks, right_blocks, alive, block_size):
    row_total = left.shape[0]
    left_parts = jnp.take(
        left.reshape(row_total, left.shape[1] // block_size, block_size), left_blocks, axis=1
    )
    right_parts = jnp.take(
        right.reshape(row_total, right.shape[1] // block_size, block_size), right_blocks, axis=1
    )
    result = jnp.einsum("rsk,rsn->skn", left_parts, right_parts, preferred_element_type=jnp.float32)
    return jnp.where(alive[:, None, None], result, 0.0).astype(jnp.bfloat16)


def on_device(
    tokens, cotangent, gate_vals, up_vals, gu_index, gu_count, down_vals, down_index, down_count
):
    block_size = gate_vals.shape[-1]
    slots_total = gate_vals.shape[2]
    wide_size = lax.axis_size("wide")
    d_blocks = tokens.shape[1] // block_size
    f_blocks = FF // (block_size * wide_size)
    f_width = f_blocks * block_size
    slot_range = jnp.arange(slots_total, dtype=jnp.int32)
    gate_alive = slot_range < gu_count[0, 0]
    down_alive = slot_range < down_count[0, 0]
    gate_rows = gu_index[0, 0] // f_blocks
    gate_cols = gu_index[0, 0] % f_blocks
    down_rows = down_index[0, 0] // d_blocks
    down_cols = down_index[0, 0] % d_blocks
    gate_tile = jnp.where(gate_alive[:, None, None], gate_vals[0, 0], 0)
    up_tile = jnp.where(gate_alive[:, None, None], up_vals[0, 0], 0)
    down_tile = jnp.where(down_alive[:, None, None], down_vals[0, 0], 0)
    paired = jnp.concatenate([gate_tile, up_tile], axis=0)
    paired_rows = jnp.concatenate([gate_rows, gate_rows], axis=0)
    paired_cols = jnp.concatenate([gate_cols, gate_cols + f_blocks], axis=0)
    paired_alive = jnp.concatenate([gate_alive, gate_alive], axis=0)
    x_all = lax.all_gather(tokens, "wide", axis=0, tiled=True)
    dy_all = lax.all_gather(cotangent, "wide", axis=0, tiled=True)
    merged = lax.psum_scatter(
        apply_blocks(x_all, paired, paired_rows, paired_cols, 2 * f_blocks, "rsk,skn->rsn"),
        "narrow",
        scatter_dimension=0,
        tiled=True,
    )
    d_hidden = lax.psum_scatter(
        apply_blocks(dy_all, down_tile, down_cols, down_rows, f_blocks, "rsn,skn->rsk"),
        "narrow",
        scatter_dimension=0,
        tiled=True,
    )
    gate_out = merged[:, :f_width]
    up_out = merged[:, f_width:]
    sigmoid_g = jax.nn.sigmoid(gate_out)
    hidden = (gate_out * sigmoid_g * up_out).astype(jnp.bfloat16)
    d_gate = (d_hidden * up_out * sigmoid_g * (1.0 + gate_out * (1.0 - sigmoid_g))).astype(
        jnp.bfloat16
    )
    d_up = (d_hidden * gate_out * sigmoid_g).astype(jnp.bfloat16)
    hidden_all, dgate_all, dup_all = (
        lax.all_gather(hidden, "narrow", axis=0, tiled=True),
        lax.all_gather(d_gate, "narrow", axis=0, tiled=True),
        lax.all_gather(d_up, "narrow", axis=0, tiled=True),
    )
    down_grad = block_grads(hidden_all, dy_all, down_rows, down_cols, down_alive, block_size)
    grads_pair = jnp.concatenate([dgate_all, dup_all], axis=1)
    both_grads = block_grads(x_all, grads_pair, paired_rows, paired_cols, paired_alive, block_size)
    gate_grad = both_grads[:slots_total]
    up_grad = both_grads[slots_total:]
    d_tokens = lax.psum_scatter(
        apply_blocks(grads_pair, paired, paired_cols, paired_rows, d_blocks, "rsn,skn->rsk"),
        "wide",
        scatter_dimension=0,
        tiled=True,
    ).astype(jnp.bfloat16)
    return (d_tokens, gate_grad[None, None], up_grad[None, None], down_grad[None, None])


def solution(mesh):
    in_specs = (
        P("wide", "narrow"),
        P("wide", "narrow"),
        P("narrow", "wide", None, None, None),
        P("narrow", "wide", None, None, None),
        P("narrow", "wide", None),
        P("narrow", "wide"),
        P("wide", "narrow", None, None, None),
        P("wide", "narrow", None),
        P("wide", "narrow"),
    )
    out_specs = (
        P("wide", "narrow"),
        P("narrow", "wide", None, None, None),
        P("narrow", "wide", None, None, None),
        P("wide", "narrow", None, None, None),
    )
    return jax.shard_map(
        on_device, mesh=mesh, in_specs=in_specs, out_specs=out_specs, check_vma=False
    )
```

profile of v0, /device:TPU:2, one launch (start us, length us, event | category | flops | bytes accessed | tf_op | source)
XLA Modules:
  0.0 692.6 jit_solution(14160900754381156844)
XLA Ops:
  7.2 0.0 all-gather.3.cloned.1.call-start
  7.2 0.7 all-gather.3.cloned.1.call-update
  7.9 0.0 all-gather.5.cloned.1.call-start
  7.9 0.7 all-gather.5.cloned.1.call-update
  8.6 0.0 reduce-scatter.10.cloned.1.call-start
  10.0 1.2 copy.61
  11.2 1.2 copy.62
  12.4 1.9 copy.63
  14.4 1.2 compare_and_fusion.3
  15.5 1.2 broadcast_add_fusion
  16.8 0.9 bitcast_select_fusion.3
  17.7 139.1 %all-gather.3.cloned.1.call-done = bf16[512,1024]{1,0:T(8,128)(2,1)} async-done(((bf16[8,1024]{1,0:T(8,128)(2,1)}), bf16[512,1024]{1,0:T(8,128)(2,1)}) %all-gather.3.cloned.1.call-update) | async-done | bytes 1048592 | tf_op jit(solution)/shard_map/all_gather | solution.py:58
  156.8 1.5 copy.64
  158.3 0.7 copy.65
  159.0 1.9 gather_fusion.1
  160.9 0.0 copy-done.5
  160.9 2.3 convolution_bitcast_fusion
  163.2 3.5 copy.67
  166.8 3.8 convolution_bitcast_fusion.2
  170.5 0.2 copy.93
  170.7 1.0 copy.95
  171.7 0.0 reduce-scatter.10.cloned.1.call-update
  171.8 0.0 reduce-scatter.12.cloned.1.call-start
  171.8 0.0 copy-done.2
  171.8 0.1 compare_and_fusion
  171.9 124.8 %all-gather.5.cloned.1.call-done = bf16[512,1024]{1,0:T(8,128)(2,1)} async-done(((bf16[8,1024]{1,0:T(8,128)(2,1)}), bf16[512,1024]{1,0:T(8,128)(2,1)}) %all-gather.5.cloned.1.call-update) | async-done | bytes 1048592 | tf_op jit(solution)/shard_map/all_gather | solution.py:57
  296.7 1.5 copy.69
  298.2 0.7 copy.70
  298.9 0.0 copy-start.1
  298.9 2.7 gather_fusion.2
  301.6 5.6 fusion.7
  307.2 6.6 copy.71
  313.8 5.1 convolution_bitcast_fusion.1
  318.9 0.4 copy.94
  319.3 1.3 copy.97
  320.6 0.0 reduce-scatter.12.cloned.1.call-update
  320.6 0.0 reduce-scatter.8.cloned.1.call-start
  320.7 0.1 pad_add_fusion.1
  320.8 18.1 %reduce-scatter.10.cloned.1.call-done = f32[64,256]{1,0:T(8,128)} async-done(((f32[512,256]{1,0:T(8,128)}), f32[64,256]{1,0:T(8,128)}) %reduce-scatter.10.cloned.1.call-update) | async-done | bytes 65552 | tf_op jit(solution)/shard_map/reduce_scatter | solution.py:65
  338.8 48.9 %reduce-scatter.12.cloned.1.call-done = f32[64,512]{1,0:T(8,128)} async-done(((f32[512,512]{1,0:T(8,128)}), f32[64,512]{1,0:T(8,128)}) %reduce-scatter.12.cloned.1.call-update) | async-done | bytes 131088 | tf_op jit(solution)/shard_map/reduce_scatter | solution.py:59
  387.8 0.9 multiply_convert_fusion.2
  388.7 28.5 %all_gather.17 = bf16[512,256]{1,0:T(8,128)(2,1)S(1)} all-gather(bf16[64,256]{1,0:T(8,128)(2,1)S(1)} %get-tuple-element.31), channel_id=1, replica_groups=mesh['wide'=64,'narrow'=8] {'narrow'}, dimensions={0}, use_global_device_ids=true | all-gather | bytes 294912 | tf_op jit(solution)/shard_map/all_gather | solution.py:81
  417.2 0.1 copy.77
  417.3 28.5 %all_gather.18 = bf16[512,256]{1,0:T(8,128)(2,1)S(1)} all-gather(bf16[64,256]{1,0:T(8,128)(2,1)S(1)} %get-tuple-element.32), channel_id=1, replica_groups=mesh['wide'=64,'narrow'=8] {'narrow'}, dimensions={0}, use_global_device_ids=true | all-gather | bytes 294912 | tf_op jit(solution)/shard_map/all_gather | solution.py:82
  445.8 0.1 copy.78
  446.0 0.3 copy.79
  446.3 2.7 gather_fusion.3
  449.0 5.7 fusion.10
  454.6 6.6 copy.81
  461.2 4.3 fusion.42
  465.5 0.0 copy-start.7
  465.5 1.8 copy.101
  467.3 0.0 reduce-scatter.8.cloned.1.call-update
  467.4 0.6 pad_add_fusion
  468.0 28.4 %all_gather.19 = bf16[512,256]{1,0:T(8,128)(2,1)S(1)} all-gather(bf16[64,256]{1,0:T(8,128)(2,1)S(1)} %get-tuple-element.33), channel_id=1, replica_groups=mesh['wide'=64,'narrow'=8] {'narrow'}, dimensions={0}, use_global_device_ids=true | all-gather | bytes 294912 | tf_op jit(solution)/shard_map/all_gather | solution.py:80
  496.4 0.1 copy.83
  496.5 0.2 copy.84
  496.7 1.9 gather_fusion
  498.6 2.8 fusion.33
  501.5 0.9 copy.87
  502.4 3.2 select_convert_fusion
  505.7 1.0 slice_bitcast_fusion
  506.6 178.1 %reduce-scatter.8.cloned.1.call-done = f32[8,1024]{1,0:T(8,128)} async-done(((f32[512,1024]{1,0:T(8,128)}), f32[8,1024]{1,0:T(8,128)}) %reduce-scatter.8.cloned.1.call-update) | async-done | bytes 32784 | tf_op jit(solution)/shard_map/reduce_scatter | solution.py:89
  684.8 1.4 convert_element_type.27
  (20 shorter events, 0.1 us)
Async XLA Ops:
  7.2 149.6 %all-gather.3.cloned.1.call-start = ((), (), s32[]{:S(2)}) async-start(), calls=%async_computation.3 | async-start | bytes 1064960 | tf_op jit(solution)/shard_map/all_gather | solution.py:58
  7.9 288.8 %all-gather.5.cloned.1.call-start = ((), (), s32[]{:S(2)}) async-start(), calls=%async_computation.4 | async-start | bytes 1064960 | tf_op jit(solution)/shard_map/all_gather | solution.py:57
  8.6 330.2 %reduce-scatter.10.cloned.1.call-start = ((), (), s32[]{:S(2)}) async-start(), calls=%async_computation.6 | async-start | bytes 589824 | tf_op jit(solution)/shard_map/reduce_scatter | solution.py:65
  14.4 146.5 %copy-start.5 = (pred[12]{0:T(512)(128)(4,1)}, pred[12]{0:T(512)(128)(4,1)S(1)}, u32[]{:S(2)}) copy-start(pred[12]{0:T(512)(128)(4,1)S(1)} %iota_compare_fusion.3) | copy-start | bytes 40
  166.8 5.1 copy-start.2
  166.8 5.1 copy-start.3
  166.8 5.1 copy-start.4
  171.8 216.0 %reduce-scatter.12.cloned.1.call-start = ((), (), s32[]{:S(2)}) async-start(), calls=%async_computation.7 | async-start | bytes 1179648 | tf_op jit(solution)/shard_map/reduce_scatter | solution.py:59
  298.9 2.7 copy-start.1
  320.6 364.1 %reduce-scatter.8.cloned.1.call-start = ((), (), s32[]{:S(2)}) async-start(), calls=%async_computation.5 | async-start | bytes 2129920 | tf_op jit(solution)/shard_map/reduce_scatter | solution.py:89
  465.5 1.9 copy-start.6
  465.5 2.4 copy-start.7
  498.6 3.8 copy-start
Sparse Core Ops, SparseCore 0:
  11.3 145.4 all-gather.2
  160.1 136.5 all-gather.4
  299.5 39.2 reduce-scatter.9
  341.5 46.1 reduce-scatter.11
  467.5 217.2 reduce-scatter.7
where the time goes:
time: 693 us
  waiting for transfers between devices  510 us (74%)
  blocking collectives  85.3 us (12%)
  local copies, waits for them, and re-layouts  42.1 us (6%)
  matrix products  32.8 us (5%)
  between operations  15.3 us (2%)
    reduce_scatter x1, waiting for transfers between devices, on_device(): lax.psum_scatter(apply_blocks(grads_pair, paired, paired_cols, paired_row...  178 us
    all_gather x1, waiting for transfers between devices, on_device(): dy_all = lax.all_gather(cotangent, 'wide', axis=0, tiled=True)  139 us
    all_gather x1, waiting for transfers between devices, on_device(): x_all = lax.all_gather(tokens, 'wide', axis=0, tiled=True)  125 us
    reduce_scatter x1, waiting for transfers between devices, on_device(): lax.psum_scatter(apply_blocks(x_all, paired, paired_rows, paired_cols, 2...  48.9 us
    all_gather x1, blocking collectives, on_device(): lax.all_gather(d_gate, 'narrow', axis=0, tiled=True)  28.5 us
    all_gather x1, blocking collectives, on_device(): lax.all_gather(d_up, 'narrow', axis=0, tiled=True)  28.5 us
    all_gather x1, blocking collectives, on_device(): lax.all_gather(hidden, 'narrow', axis=0, tiled=True)  28.4 us
    reduce_scatter x1, waiting for transfers between devices, on_device(): lax.psum_scatter(apply_blocks(dy_all, down_tile, down_cols, down_rows, f_...  18.1 us
  transfers between devices with their start and end apart: 5, of which 5 were waited for; matrix products, arithmetic and copies ran while one was open for 8% of the time, Pallas kernels for 0%

commit v1 on v0

--- a/solution.py
+++ b/solution.py
@@ -54,7 +54,15 @@
     paired_rows = jnp.concatenate([gate_rows, gate_rows], axis=0)
     paired_cols = jnp.concatenate([gate_cols, gate_cols + f_blocks], axis=0)
     paired_alive = jnp.concatenate([gate_alive, gate_alive], axis=0)
-    x_all = lax.all_gather(tokens, "wide", axis=0, tiled=True)
+    x_all = jnp.concatenate(
+        lax.all_to_all(
+            jnp.stack([tokens for _ in range(lax.axis_size("wide"))], 0),
+            axis_name="wide",
+            split_axis=0,
+            concat_axis=0,
+        ),
+        axis=0,
+    )
     dy_all = lax.all_gather(cotangent, "wide", axis=0, tiled=True)
     merged = lax.psum_scatter(
         apply_blocks(x_all, paired, paired_rows, paired_cols, 2 * f_blocks, "rsk,skn->rsn"),

time: 693 us -> 584 us (0.84)
  the two profiles are of different devices: /device:TPU:2 before, /device:TPU:4 now
where the time goes in v1:
time: 584 us; the launch traced here: 583 us
  waiting for transfers between devices  386 us (66%)
  blocking collectives  84.8 us (15%)
  local copies, waits for them, and re-layouts  40.5 us (7%)
  matrix products  32.8 us (6%)
  starting transfers between devices  19.2 us (3%)
  between operations  15.4 us (3%)
    reduce_scatter x1, waiting for transfers between devices, on_device(): lax.psum_scatter(apply_blocks(grads_pair, paired, paired_cols, paired_row...  179 us
    all_gather x1, waiting for transfers between devices, on_device(): dy_all = lax.all_gather(cotangent, 'wide', axis=0, tiled=True)  141 us
    reduce_scatter x1, waiting for transfers between devices, on_device(): lax.psum_scatter(apply_blocks(x_all, paired, paired_rows, paired_cols, 2...  49.8 us
    all_gather x1, blocking collectives, on_device(): lax.all_gather(d_up, 'narrow', axis=0, tiled=True)  28.6 us
    all_gather x1, blocking collectives, on_device(): lax.all_gather(hidden, 'narrow', axis=0, tiled=True)  28.4 us
    all_gather x1, blocking collectives, on_device(): lax.all_gather(d_gate, 'narrow', axis=0, tiled=True)  27.8 us
    all_to_all x1, starting transfers between devices, on_device(): lax.all_to_all(jnp.stack([tokens for _ in range(lax.axis_size('wide'))],...  19 us
    transpose x3, local copies, waits for them, and re-layouts, apply_blocks(): jnp.einsum(form, picked, tile_values, preferred_element_type=jnp.float32)  16.7 us
  transfers between devices with their start and end apart: 5, of which 4 were waited for; matrix products, arithmetic and copies ran while one was open for 9% of the time, Pallas kernels for 0%

profile of v1, /device:TPU:4, one launch (start us, length us, event | category | flops | bytes accessed | tf_op | source)
XLA Modules:
  0.0 583.5 jit_solution(12646750919811987706)
XLA Ops:
  7.2 0.0 copy-start.10
  7.2 1.9 stack.2
  9.1 19.0 %all-to-all-start = ((bf16[64,8,1024]{2,1,0:T(8,128)(2,1)}), bf16[64,8,1024]{2,1,0:T(8,128)(2,1)}, u32[]{:S(2)}, u32[]{:S(2)}) async-start(bf16[64,8,1024]{2,1,0:T(8,128)(2,1)} %stack.2), calls=%async_computation | async-start | bytes 2097152 | tf_op jit(solution)/shard_map/all_to_all | solution.py:58
  28.1 0.0 all-gather.2.cloned.1.call-start
  28.2 0.7 all-gather.2.cloned.1.call-update
  28.9 0.0 reduce-scatter.10.cloned.1.call-start
  30.2 0.2 copy.59
  30.5 0.2 copy.60
  30.7 0.9 copy.61
  31.7 0.5 compare_and_fusion.3
  32.2 0.6 broadcast_add_fusion
  32.8 0.9 bitcast_select_fusion.3
  33.7 141.4 %all-gather.2.cloned.1.call-done = bf16[512,1024]{1,0:T(8,128)(2,1)} async-done(((bf16[8,1024]{1,0:T(8,128)(2,1)}), bf16[512,1024]{1,0:T(8,128)(2,1)}) %all-gather.2.cloned.1.call-update) | async-done | bytes 1048592 | tf_op jit(solution)/shard_map/all_gather | solution.py:66
  175.1 1.5 copy.62
  176.6 0.7 copy.63
  177.2 1.9 gather_fusion.1
  179.2 2.3 convolution_bitcast_fusion
  181.5 3.5 copy.65
  185.0 3.8 convolution_bitcast_fusion.2
  188.8 0.2 copy.90
  189.0 1.0 copy.92
  190.0 0.0 reduce-scatter.10.cloned.1.call-update
  190.1 0.0 reduce-scatter.12.cloned.1.call-start
  190.1 0.1 compare_and_fusion
  190.2 0.0 all-to-all-done
  190.2 1.5 copy.96
  191.7 0.1 copy.67
  191.9 0.0 copy-start.1
  191.9 2.7 gather_fusion.2
  194.6 0.0 copy-done.1
  194.6 5.6 fusion.7
  200.2 6.6 %copy.68 = f32[512,24,128]{2,1,0:T(8,128)} copy(f32[512,24,128]{0,2,1:T(8,128)} %fusion.7) | data formatting | bytes 12582912 | tf_op jit(solution)/shard_map/rsk,skn->rsn/transpose | solution.py:14
  206.8 5.1 convolution_bitcast_fusion.1
  211.9 0.4 copy.91
  212.3 1.3 copy.94
  213.6 0.0 reduce-scatter.12.cloned.1.call-update
  213.6 0.0 reduce-scatter.8.cloned.1.call-start
  213.7 0.1 pad_add_fusion.1
  213.8 14.2 %reduce-scatter.10.cloned.1.call-done = f32[64,256]{1,0:T(8,128)} async-done(((f32[512,256]{1,0:T(8,128)}), f32[64,256]{1,0:T(8,128)}) %reduce-scatter.10.cloned.1.call-update) | async-done | bytes 65552 | tf_op jit(solution)/shard_map/reduce_scatter | solution.py:73
  228.0 49.8 %reduce-scatter.12.cloned.1.call-done = f32[64,512]{1,0:T(8,128)} async-done(((f32[512,512]{1,0:T(8,128)}), f32[64,512]{1,0:T(8,128)}) %reduce-scatter.12.cloned.1.call-update) | async-done | bytes 131088 | tf_op jit(solution)/shard_map/reduce_scatter | solution.py:67
  277.8 0.9 multiply_convert_fusion.2
  278.7 27.8 %all_gather.13 = bf16[512,256]{1,0:T(8,128)(2,1)S(1)} all-gather(bf16[64,256]{1,0:T(8,128)(2,1)S(1)} %get-tuple-element.31), channel_id=1, replica_groups=mesh['wide'=64,'narrow'=8] {'narrow'}, dimensions={0}, use_global_device_ids=true | all-gather | bytes 294912 | tf_op jit(solution)/shard_map/all_gather | solution.py:89
  306.5 0.1 copy.74
  306.7 28.6 %all_gather.14 = bf16[512,256]{1,0:T(8,128)(2,1)S(1)} all-gather(bf16[64,256]{1,0:T(8,128)(2,1)S(1)} %get-tuple-element.32), channel_id=1, replica_groups=mesh['wide'=64,'narrow'=8] {'narrow'}, dimensions={0}, use_global_device_ids=true | all-gather | bytes 294912 | tf_op jit(solution)/shard_map/all_gather | solution.py:90
  335.3 0.1 copy.75
  335.5 0.3 copy.76
  335.8 2.7 gather_fusion.3
  338.5 5.7 fusion.10
  344.1 6.6 %copy.78 = f32[512,24,128]{2,1,0:T(8,128)} copy(f32[512,24,128]{0,2,1:T(8,128)} %fusion.10) | data formatting | bytes 12582912 | tf_op jit(solution)/shard_map/rsn,skn->rsk/transpose | solution.py:14
  350.7 4.3 fusion.42
  355.0 0.0 copy-start.11
  355.0 1.8 copy.99
  356.8 0.0 reduce-scatter.8.cloned.1.call-update
  356.9 0.6 pad_add_fusion
  357.5 28.4 %all_gather.15 = bf16[512,256]{1,0:T(8,128)(2,1)S(1)} all-gather(bf16[64,256]{1,0:T(8,128)(2,1)S(1)} %get-tuple-element.33), channel_id=1, replica_groups=mesh['wide'=64,'narrow'=8] {'narrow'}, dimensions={0}, use_global_device_ids=true | all-gather | bytes 294912 | tf_op jit(solution)/shard_map/all_gather | solution.py:88
  385.9 0.1 copy.80
  386.0 0.2 copy.81
  386.2 1.9 gather_fusion
  388.2 2.8 fusion.33
  391.0 0.9 copy.84
  391.9 3.2 select_convert_fusion
  395.2 1.0 slice_bitcast_fusion
  396.1 179.4 %reduce-scatter.8.cloned.1.call-done = f32[8,1024]{1,0:T(8,128)} async-done(((f32[512,1024]{1,0:T(8,128)}), f32[8,1024]{1,0:T(8,128)}) %reduce-scatter.8.cloned.1.call-update) | async-done | bytes 32784 | tf_op jit(solution)/shard_map/reduce_scatter | solution.py:97
  575.6 1.4 convert_element_type.27
  (30 shorter events, 0.1 us)
Async XLA Ops:
  7.2 23.0 %copy-start.2 = (bf16[1,1,12,128,128]{4,3,2,1,0:T(8,128)(2,1)S(1)}, bf16[1,1,12,128,128]{4,3,2,1,0:T(8,128)(2,1)}, u32[]{:S(2)}) copy-start(bf16[1,1,12,128,128]{4,3,2,1,0:T(8,128)(2,1)} %param.17) | copy-start | bytes 1179652
  7.2 23.3 %copy-start.3 = (bf16[1,1,12,128,128]{4,3,2,1,0:T(8,128)(2,1)S(1)}, bf16[1,1,12,128,128]{4,3,2,1,0:T(8,128)(2,1)}, u32[]{:S(2)}) copy-start(bf16[1,1,12,128,128]{4,3,2,1,0:T(8,128)(2,1)} %param.18) | copy-start | bytes 1179652
  7.2 23.5 %copy-start.4 = (bf16[1,1,12,128,128]{4,3,2,1,0:T(8,128)(2,1)S(1)}, bf16[1,1,12,128,128]{4,3,2,1,0:T(8,128)(2,1)}, u32[]{:S(2)}) copy-start(bf16[1,1,12,128,128]{4,3,2,1,0:T(8,128)(2,1)} %param.21) | copy-start | bytes 1179652
  7.2 24.5 %copy-start.10 = (s32[1,1,12]{2,1,0:T(1,128)S(1)}, s32[1,1,12]{2,1,0:T(1,128)}, u32[]{:S(2)}) copy-start(s32[1,1,12]{2,1,0:T(1,128)} %param.22) | copy-start | bytes 148
  7.2 25.0 %copy-start.12 = (s32[1,1,12]{2,1,0:T(1,128)S(1)}, s32[1,1,12]{2,1,0:T(1,128)}, u32[]{:S(2)}) copy-start(s32[1,1,12]{2,1,0:T(1,128)} %param.19) | copy-start | bytes 148
  9.1 181.1 %all-to-all-start = ((bf16[64,8,1024]{2,1,0:T(8,128)(2,1)}), bf16[64,8,1024]{2,1,0:T(8,128)(2,1)}, u32[]{:S(2)}, u32[]{:S(2)}) async-start(bf16[64,8,1024]{2,1,0:T(8,128)(2,1)} %stack.2), calls=%async_computation | async-start | bytes 2097152 | tf_op jit(solution)/shard_map/all_to_all | solution.py:58
  28.1 146.9 %all-gather.2.cloned.1.call-start = ((), (), s32[]{:S(2)}) async-start(), calls=%async_computation.4 | async-start | bytes 1064960 | tf_op jit(solution)/shard_map/all_gather | solution.py:66
  28.9 199.1 %reduce-scatter.10.cloned.1.call-start = ((), (), s32[]{:S(2)}) async-start(), calls=%async_computation.6 | async-start | bytes 589824 | tf_op jit(solution)/shard_map/reduce_scatter | solution.py:73
  31.6 147.5 %copy-start.8 = (pred[12]{0:T(512)(128)(4,1)}, pred[12]{0:T(512)(128)(4,1)S(1)}, u32[]{:S(2)}) copy-start(pred[12]{0:T(512)(128)(4,1)S(1)} %iota_compare_fusion.3) | copy-start | bytes 40
  185.0 5.1 copy-start.5
  185.0 5.1 copy-start.6
  185.0 5.1 copy-start.7
  190.1 87.7 %reduce-scatter.12.cloned.1.call-start = ((), (), s32[]{:S(2)}) async-start(), calls=%async_computation.7 | async-start | bytes 1179648 | tf_op jit(solution)/shard_map/reduce_scatter | solution.py:67
  191.9 2.7 copy-start.1
  213.6 361.9 %reduce-scatter.8.cloned.1.call-start = ((), (), s32[]{:S(2)}) async-start(), calls=%async_computation.5 | async-start | bytes 2129920 | tf_op jit(solution)/shard_map/reduce_scatter | solution.py:97
  355.0 1.9 copy-start.9
  355.0 2.4 copy-start.11
  388.2 3.8 copy-start
Sparse Core Ops, SparseCore 0:
  32.2 142.7 all-gather.1
  190.2 37.7 reduce-scatter.9
  230.8 46.9 reduce-scatter.11
  357.0 218.5 reduce-scatter.7
